TPU v7x, 512 devices: a whole 4x4x16 slice. The times are simulated.
512 devices in a mesh: dp: 64 (over x, z_lo, core), mp: 8 (over y, z_hi).
Axes of the slice: x: 4, y: 4, z: 16 (z_hi: 2, z_lo: 8; z = z_hi * 8 + z_lo), core: 2. Of those that a mesh axis runs over, the one named last changes fastest.
Arguments:
- master: float32 [8, 256, 512], P('mp', 'dp'), may hold values from -4 to 4
- moment: float32 [8, 256, 512], P('mp', 'dp'), may hold values from -0.06 to 0.06
- variance: float32 [8, 256, 512], P('mp', 'dp'), may hold values from 3e-06 to 3e-05
- flat_slot: int32 [256], replicated, may hold values from 0 to 255, each once
- feedback: bfloat16 [64, 2, 64, 8192], P('dp', None, 'mp'), may hold values from -0.029907227 to 0.029907227
- activations: bfloat16 [2, 8192, 8192], P(None, ('dp', 'mp')), may hold values from -24 to 24
- output_grads: bfloat16 [2, 8192, 8192], P(None, ('dp', 'mp')), may hold values from -24 to 24
Outputs:
- master_out: float32 [8, 256, 512], P('mp', 'dp')
- moment_out: float32 [8, 256, 512], P('mp', 'dp')
- feedback_out: bfloat16 [64, 2, 64, 8192], P('dp', None, 'mp')
Inputs may be any that keep to these rules, and one draw needn't show every extreme that they name: `flat_slot`: every position of the flat buffer holds exactly one of the 256 segments.
All inputs are finite; a program needn't handle non-finite values. Where the computation divides by a largest or mean magnitude, that divisor is 1e-20 or more.
Results may differ from a plain program's by a relative error of at most 0.0036.
The roundings to bfloat16 on the way count: a program that leaves them out, or rounds other values in their place, can miss the bound.
Values may be sent and summed in bfloat16 or wider, within the bound.
A program may use at most 64 MiB of HBM per device.

v0:
```python
import jax
import jax.numpy as jnp
from jax import lax
from jax.sharding import PartitionSpec as P

beta_one = 0.9
step_rate = 0.05
epsilon = 1e-08
down_scale = 28672.0 ** (-0.5)


def silu_slope(preact):
    sigmoid_value = jax.nn.sigmoid(preact)
    return sigmoid_value * (1.0 + preact * (1.0 - sigmoid_value))


def gradients(weights, inputs, cotangent, model_width):
    up_scale = model_width ** (-0.5)
    before = up_scale * jnp.dot(inputs, weights[0].T, preferred_element_type=jnp.float32)
    hidden = jax.nn.silu(before).astype(jnp.bfloat16)
    back_grad = down_scale * jnp.dot(cotangent, weights[1].T, preferred_element_type=jnp.float32)
    slope_grad = (back_grad * silu_slope(before)).astype(jnp.bfloat16)
    grad_up = up_scale * jnp.dot(slope_grad.T, inputs, preferred_element_type=jnp.float32)
    grad_down = down_scale * jnp.dot(hidden.T, cotangent, preferred_element_type=jnp.float32)
    return jnp.stack([grad_up, grad_down])


def per_device(master, moment, variance, flat_slot, feedback, activations, output_grads):
    owner_rows = master.shape[1]
    total_rows = flat_slot.shape[0]
    hidden_rows = feedback.shape[2]
    model_width = feedback.shape[3]
    workers = lax.axis_size("dp")
    tensor_shape = (2, hidden_rows, model_width)
    segment_shape = (total_rows, master.shape[2])
    inverse = (
        jnp.zeros((total_rows,), jnp.int32)
        .at[flat_slot]
        .set(jnp.arange(total_rows, dtype=jnp.int32))
    )
    working_flat = lax.all_gather(master[0].astype(jnp.bfloat16), "dp", axis=0, tiled=True)
    moment_flat, variance_flat = (
        lax.all_gather(moment[0], "dp", axis=0, tiled=True),
        lax.all_gather(variance[0], "dp", axis=0, tiled=True),
    )
    working = working_flat[flat_slot].reshape(tensor_shape)
    moment_t = moment_flat[flat_slot].reshape(tensor_shape)
    denominator = jnp.sqrt(variance_flat[flat_slot].reshape(tensor_shape)) + epsilon
    group_inputs, group_grads = (
        lax.all_gather(activations, "mp", axis=1, tiled=True),
        lax.all_gather(output_grads, "mp", axis=1, tiled=True),
    )
    step_one = gradients(working, group_inputs[0], group_grads[0], model_width)
    local_moment = beta_one * moment_t + (1.0 - beta_one) * step_one
    local_weights = (working.astype(jnp.float32) - step_rate * local_moment / denominator).astype(
        jnp.bfloat16
    )
    step_two = gradients(local_weights, group_inputs[1], group_grads[1], model_width)
    shifted = local_moment + feedback[0].astype(jnp.float32)
    magnitude = jnp.mean(jnp.abs(shifted), axis=-1, keepdims=True) + 1e-06
    packed = magnitude * jnp.tanh(shifted / magnitude)
    new_error = (shifted - packed).astype(jnp.bfloat16)
    first_row = lax.axis_index("dp") * owner_rows
    grad_flat = step_two.reshape(segment_shape)[inverse]
    moment_whole = lax.psum(packed, "dp")
    own_segments = lax.dynamic_slice_in_dim(inverse, first_row, owner_rows, 0)
    moment_own = moment_whole.reshape(segment_shape)[own_segments]
    grad_own = lax.psum_scatter(grad_flat, "dp", scatter_dimension=0, tiled=True)
    mean_moment = moment_own / workers
    mean_grad = grad_own / workers
    moment_new = beta_one * mean_moment + (1.0 - beta_one) * mean_grad
    owner_denominator = jnp.sqrt(variance[0]) + epsilon
    master_new = master[0] - step_rate * (mean_moment + moment_new) / owner_denominator
    return (master_new[None], moment_new[None], new_error[None])


def solution(mesh):
    in_specs = (
        P("mp", "dp", None),
        P("mp", "dp", None),
        P("mp", "dp", None),
        P(),
        P("dp", None, "mp", None),
        P(None, ("dp", "mp"), None),
        P(None, ("dp", "mp"), None),
    )
    out_specs = (P("mp", "dp", None), P("mp", "dp", None), P("dp", None, "mp", None))
    return jax.shard_map(
        per_device, mesh=mesh, in_specs=in_specs, out_specs=out_specs, check_vma=False
    )
```

profile of v0, /device:TPU:1, one launch (start us, length us, event | category | flops | bytes accessed | tf_op | source)
XLA Modules:
  0.0 1362.9 jit_solution(14703939547487024372)
XLA Ops:
  7.9 0.7 all-gather.6.cloned.1.call-update
  8.7 0.7 copy.10
  9.4 181.0 %all-gather = f32[1,256,512]{2,0,1:T(1,128)S(1)} all-gather(f32[1,4,512]{2,0,1:T(1,128)S(1)} %copy.10), channel_id=2, replica_groups=mesh['dp'=64,'mp'=8] {'dp'}, dimensions={1}, use_global_device_ids=true | all-gather | bytes 532480 | tf_op jit(solution)/shard_map/all_gather | solution.py:43
  190.5 0.7 compare_select_fusion.1
  191.2 1.0 gather_fusion
  192.4 172.0 %all-gather.2 = bf16[64,4,512]{2,1,0:T(4,128)(2,1)S(1)} all-gather(bf16[1,4,512]{2,1,0:T(4,128)(2,1)S(1)} %fusion.24), channel_id=1, replica_groups=mesh['dp'=64,'mp'=8] {'dp'}, dimensions={0}, use_global_device_ids=true | all-gather | bytes 266240 | tf_op jit(solution)/shard_map/all_gather | solution.py:41
  364.5 1.2 gather_fusion.1
  365.8 114.9 %all-gather.1 = f32[1,256,512]{2,0,1:T(1,128)S(1)} all-gather(f32[1,4,512]{2,0,1:T(1,128)S(1)} %copy.11), channel_id=3, replica_groups=mesh['dp'=64,'mp'=8] {'dp'}, dimensions={1}, use_global_device_ids=true | all-gather | bytes 532480 | tf_op jit(solution)/shard_map/all_gather | solution.py:44
  480.7 1.0 gather_fusion.3
  482.1 1.4 scatter_custom_fusion
  483.5 1.3 dynamic-slice
  485.6 2.3 fusion.12
  487.8 2.0 convolution_multiply_fusion.2
  489.8 3.8 convolution_multiply_fusion.3
  493.8 0.9 subtract_convert_fusion.1
  494.8 0.9 reshape.80
  495.7 2.3 fusion.7
  498.0 2.0 fusion
  500.0 3.8 fusion.1
  503.9 1.8 gather_fusion.4
  505.8 0.9 subtract_convert_fusion
  506.6 846.8 %all-reduce.4.cloned.1.call-done = (f32[256,512]{1,0:T(8,128)}, f32[256,512]{1,0:T(8,128)}) async-done(((f32[256,512]{1,0:T(8,128)}, f32[256,512]{1,0:T(8,128)}), (f32[256,512]{1,0:T(8,128)}, f32[256,512]{1,0:T(8,128)})) %all-reduce.4.cloned.1.call-update) | async-done | bytes 1048592 | tf_op jit(solution)/shard_map/psum | solution.py:65
  1353.5 1.6 gather_fusion.2
  1355.1 1.3 fusion.33
  (39 shorter events, 2.2 us)
Async XLA Ops:
  7.2 478.4 %all-gather.8.cloned.1.call-start = ((), (), s32[]{:S(2)}) async-start(), calls=%async_computation.1 | async-start | bytes 4718592 | tf_op jit(solution)/shard_map/all_gather | solution.py:50
  7.9 480.0 %all-gather.6.cloned.1.call-start = ((), (), s32[]{:S(2)}) async-start(), calls=%async_computation | async-start | bytes 4718592 | tf_op jit(solution)/shard_map/all_gather | solution.py:51
  8.6 1344.8 %all-reduce.4.cloned.1.call-start = ((), (), s32[]{:S(2)}) async-start(), calls=%async_computation.2 | async-start | bytes 2097152 | tf_op jit(solution)/shard_map/psum | solution.py:65
  190.5 2.0 copy-start.2
  192.1 173.6 %copy-start.3 = (f32[1,4,512]{2,1,0:T(4,128)S(1)}, f32[1,4,512]{2,1,0:T(4,128)}, u32[]{:S(2)}) copy-start(f32[1,4,512]{2,1,0:T(4,128)} %param.9) | copy-start | bytes 24580
  485.5 8.1 copy-start
  494.8 5.2 copy-start.1
Sparse Core Ops, SparseCore 0:
  11.2 185.7 all-gather.7
  200.2 170.1 all-gather.5
  505.9 847.5 all-reduce.3
where the time goes:
time: 1360 us
  waiting for transfers between devices  848 us (62%)
  blocking collectives  468 us (34%)
  matrix products  16.1 us (1%)
  between operations  14.6 us (1%)
    psum x1, waiting for transfers between devices, per_device(): moment_whole = lax.psum(packed, 'dp')  847 us
    all_gather x1, blocking collectives, per_device(): lax.all_gather(moment[0], 'dp', axis=0, tiled=True)  181 us
    all_gather x1, blocking collectives, per_device(): lax.all_gather(master[0].astype(jnp.bfloat16), 'dp', axis=0, tiled=True)  172 us
    all_gather x1, blocking collectives, per_device(): lax.all_gather(variance[0], 'dp', axis=0, tiled=True)  115 us
  transfers between devices with their start and end apart: 3, of which 1 were waited for; matrix products, arithmetic and copies ran while one was open for 1% of the time, Pallas kernels for 0%

commit v1 on v0

--- a/solution.py
+++ b/solution.py
@@ -38,7 +38,12 @@
         .at[flat_slot]
         .set(jnp.arange(total_rows, dtype=jnp.int32))
     )
-    working_flat = lax.all_gather(master[0].astype(jnp.bfloat16), "dp", axis=0, tiled=True)
+    working_flat = jnp.concatenate(
+        lax.all_to_all(
+            jnp.stack([master[0].astype(jnp.bfloat16)] * lax.axis_size("dp")), "dp", 0, 0
+        ),
+        axis=0,
+    )
     moment_flat, variance_flat = (
         lax.all_gather(moment[0], "dp", axis=0, tiled=True),
         lax.all_gather(variance[0], "dp", axis=0, tiled=True),

time: 1360 us -> 1260 us (0.926)
  blocking collectives: 468 us -> 341 us
  starting transfers between devices: 0.11 us -> 17.2 us
    all_gather x1 -> x0, blocking collectives: 172 us -> none  [per_device(): lax.all_gather(master[0].astype(jnp.bfloat16), 'dp', axis=0, tiled=True)]
    all_gather x1, blocking collectives: 115 us -> 174 us  [per_device(): lax.all_gather(variance[0], 'dp', axis=0, tiled=True)]
    all_to_all x0 -> x1, starting transfers between devices: none -> 17 us  [per_device(): lax.all_to_all(jnp.stack([master[0].astype(jnp.bfloat16)] * lax.axis_size...]
  transfers between devices with their start and end apart: 3 -> 4, of which waited for: 1 -> 1; matrix products, arithmetic and copies ran while one was open for 1% -> 1% of each run, Pallas kernels for 0% -> 0%
where the time goes in v1:
time: 1260 us
  waiting for transfers between devices  848 us (67%)
  blocking collectives  341 us (27%)
  starting transfers between devices  17.2 us (1%)
  matrix products  16.1 us (1%)
  between operations  14.6 us (1%)
    psum x1, waiting for transfers between devices, per_device(): moment_whole = lax.psum(packed, 'dp')  847 us
    all_gather x1, blocking collectives, per_device(): lax.all_gather(variance[0], 'dp', axis=0, tiled=True)  174 us
    all_gather x1, blocking collectives, per_device(): lax.all_gather(moment[0], 'dp', axis=0, tiled=True)  167 us
  transfers between devices with their start and end apart: 4, of which 1 were waited for; matrix products, arithmetic and copies ran while one was open for 1% of the time, Pallas kernels for 0%

profile of v1, /device:TPU:1, one launch (start us, length us, event | category | flops | bytes accessed | tf_op | source)
XLA Modules:
  0.0 1255.2 jit_solution(12530627213712996668)
XLA Ops:
  8.6 0.7 convert_bitcast_fusion.1
  9.3 0.8 stack.23
  10.1 17.0 %all-to-all-start = ((bf16[64,4,512]{2,1,0:T(4,128)(2,1)}), bf16[64,4,512]{2,1,0:T(4,128)(2,1)S(1)}, u32[]{:S(2)}, u32[]{:S(2)}) async-start(bf16[64,4,512]{2,1,0:T(4,128)(2,1)} %stack.23), calls=%async_computation | async-start | bytes 524288 | tf_op jit(solution)/shard_map/all_to_all | solution.py:42
  27.2 0.7 copy.10
  27.9 167.4 %all-gather = f32[1,256,512]{2,0,1:T(1,128)S(1)} all-gather(f32[1,4,512]{2,0,1:T(1,128)S(1)} %copy.10), channel_id=2, replica_groups=mesh['dp'=64,'mp'=8] {'dp'}, dimensions={1}, use_global_device_ids=true | all-gather | bytes 532480 | tf_op jit(solution)/shard_map/all_gather | solution.py:48
  196.1 1.0 gather_fusion
  197.4 174.0 %all-gather.1 = f32[1,256,512]{2,0,1:T(1,128)S(1)} all-gather(f32[1,4,512]{2,0,1:T(1,128)S(1)} %copy.11), channel_id=3, replica_groups=mesh['dp'=64,'mp'=8] {'dp'}, dimensions={1}, use_global_device_ids=true | all-gather | bytes 532480 | tf_op jit(solution)/shard_map/all_gather | solution.py:49
  371.4 1.0 gather_fusion.3
  372.7 1.4 scatter_custom_fusion
  374.1 1.3 dynamic-slice
  376.2 1.2 gather_fusion.1
  377.7 2.3 fusion.12
  379.9 2.0 convolution_multiply_fusion.2
  381.9 3.8 convolution_multiply_fusion.3
  385.9 0.9 subtract_convert_fusion.1
  386.9 0.9 reshape.85
  387.8 2.3 fusion.7
  390.1 2.0 fusion
  392.1 3.8 fusion.1
  396.0 1.8 gather_fusion.4
  397.8 0.9 subtract_convert_fusion
  398.7 847.0 %all-reduce.4.cloned.1.call-done = (f32[256,512]{1,0:T(8,128)}, f32[256,512]{1,0:T(8,128)}) async-done(((f32[256,512]{1,0:T(8,128)}, f32[256,512]{1,0:T(8,128)}), (f32[256,512]{1,0:T(8,128)}, f32[256,512]{1,0:T(8,128)})) %all-reduce.4.cloned.1.call-update) | async-done | bytes 1048592 | tf_op jit(solution)/shard_map/psum | solution.py:70
  1245.7 1.6 gather_fusion.2
  1247.3 1.3 fusion.32
  (41 shorter events, 3.6 us)
Async XLA Ops:
  7.2 370.5 %all-gather.7.cloned.1.call-start = ((), (), s32[]{:S(2)}) async-start(), calls=%async_computation.2 | async-start | bytes 4718592 | tf_op jit(solution)/shard_map/all_gather | solution.py:55
  7.9 372.1 %all-gather.5.cloned.1.call-start = ((), (), s32[]{:S(2)}) async-start(), calls=%async_computation.1 | async-start | bytes 4718592 | tf_op jit(solution)/shard_map/all_gather | solution.py:56
  10.1 366.0 %all-to-all-start = ((bf16[64,4,512]{2,1,0:T(4,128)(2,1)}), bf16[64,4,512]{2,1,0:T(4,128)(2,1)S(1)}, u32[]{:S(2)}, u32[]{:S(2)}) async-start(bf16[64,4,512]{2,1,0:T(4,128)(2,1)} %stack.23), calls=%async_computation | async-start | bytes 524288 | tf_op jit(solution)/shard_map/all_to_all | solution.py:42
  27.2 1218.5 %all-reduce.4.cloned.1.call-start = ((), (), s32[]{:S(2)}) async-start(), calls=%async_computation.3 | async-start | bytes 2097152 | tf_op jit(solution)/shard_map/psum | solution.py:70
  195.4 2.0 copy-start.3
  377.6 8.1 copy-start
  386.9 5.2 copy-start.1
  395.9 851.4 %copy-start.2 = (f32[1,4,512]{2,1,0:T(4,128)S(1)}, f32[1,4,512]{2,1,0:T(4,128)}, u32[]{:S(2)}) copy-start(f32[1,4,512]{2,1,0:T(4,128)} %param.7) | copy-start | bytes 24580
Sparse Core Ops, SparseCore 0:
  11.2 188.6 all-gather.6
  203.1 171.2 all-gather.4
  398.0 847.7 all-reduce.3

commit v2 on v0

--- a/solution.py
+++ b/solution.py
@@ -62,7 +62,7 @@
     new_error = (shifted - packed).astype(jnp.bfloat16)
     first_row = lax.axis_index("dp") * owner_rows
     grad_flat = step_two.reshape(segment_shape)[inverse]
-    moment_whole = lax.psum(packed, "dp")
+    moment_whole = jnp.sum(lax.all_gather(packed, "dp"), axis=0)
     own_segments = lax.dynamic_slice_in_dim(inverse, first_row, owner_rows, 0)
     moment_own = moment_whole.reshape(segment_shape)[own_segments]
     grad_own = lax.psum_scatter(grad_flat, "dp", scatter_dimension=0, tiled=True)

time: 1360 us -> 1550 us (1.14)
  waiting for transfers between devices: 848 us -> 1020 us
    psum x1 -> x0, waiting for transfers between devices: 847 us -> none  [per_device(): moment_whole = lax.psum(packed, 'dp')]
    unnamed x3 -> x5, waiting for transfers between devices: 1.39 us -> 826 us
    all_gather x0 -> x1, waiting for transfers between devices: none -> 194 us  [per_device(): moment_whole = jnp.sum(lax.all_gather(packed, 'dp'), axis=0)]
  transfers between devices with their start and end apart: 3 -> 4, of which waited for: 1 -> 2; matrix products, arithmetic and copies ran while one was open for 1% -> 2% of each run, Pallas kernels for 0% -> 0%
where the time goes in v2:
time: 1550 us; the launch traced here: 1540 us
  waiting for transfers between devices  1020 us (66%)
  blocking collectives  469 us (30%)
  matrix products  16.1 us (1%)
    unnamed x5, waiting for transfers between devices  826 us
    all_gather x1, waiting for transfers between devices, per_device(): moment_whole = jnp.sum(lax.all_gather(packed, 'dp'), axis=0)  194 us
    all_gather x1, blocking collectives, per_device(): lax.all_gather(moment[0], 'dp', axis=0, tiled=True)  183 us
    all_gather x1, blocking collectives, per_device(): lax.all_gather(master[0].astype(jnp.bfloat16), 'dp', axis=0, tiled=True)  171 us
    all_gather x1, blocking collectives, per_device(): lax.all_gather(variance[0], 'dp', axis=0, tiled=True)  115 us
  transfers between devices with their start and end apart: 4, of which 2 were waited for; matrix products, arithmetic and copies ran while one was open for 2% of the time, Pallas kernels for 0%

profile of v2, /device:TPU:1, one launch (start us, length us, event | category | flops | bytes accessed | tf_op | source)
XLA Modules:
  0.0 1544.7 jit_solution(12941746847995815206)
XLA Ops:
  7.2 0.7 all-gather.9.cloned.1.call-update
  7.9 0.7 all-gather.7.cloned.1.call-update
  8.7 0.7 copy.10
  9.4 183.4 %all-gather = f32[1,256,512]{2,0,1:T(1,128)S(1)} all-gather(f32[1,4,512]{2,0,1:T(1,128)S(1)} %copy.10), channel_id=2, replica_groups=mesh['dp'=64,'mp'=8] {'dp'}, dimensions={1}, use_global_device_ids=true | all-gather | bytes 532480 | tf_op jit(solution)/shard_map/all_gather | solution.py:43
  192.9 0.7 compare_select_fusion.1
  193.6 1.0 gather_fusion
  194.9 171.0 %all-gather.2 = bf16[64,4,512]{2,1,0:T(4,128)(2,1)S(1)} all-gather(bf16[1,4,512]{2,1,0:T(4,128)(2,1)S(1)} %fusion.26), channel_id=1, replica_groups=mesh['dp'=64,'mp'=8] {'dp'}, dimensions={0}, use_global_device_ids=true | all-gather | bytes 266240 | tf_op jit(solution)/shard_map/all_gather | solution.py:41
  365.9 1.2 gather_fusion.1
  367.4 114.7 %all-gather.1 = f32[1,256,512]{2,0,1:T(1,128)S(1)} all-gather(f32[1,4,512]{2,0,1:T(1,128)S(1)} %copy.11), channel_id=3, replica_groups=mesh['dp'=64,'mp'=8] {'dp'}, dimensions={1}, use_global_device_ids=true | all-gather | bytes 532480 | tf_op jit(solution)/shard_map/all_gather | solution.py:44
  482.1 1.0 gather_fusion.3
  483.3 2.3 fusion.12
  485.6 2.0 convolution_multiply_fusion.2
  487.6 3.8 convolution_multiply_fusion.3
  491.6 1.0 subtract_convert_fusion
  492.8 1.4 scatter_custom_fusion
  494.2 2.2 fusion.7
  496.4 2.0 fusion
  498.4 3.8 fusion.1
  502.3 1.8 gather_fusion.4
  504.2 1.3 dynamic-slice
  506.2 193.9 %all-gather.11.cloned.1.call-done = f32[64,2,8,8192]{3,2,1,0:T(8,128)} async-done(((f32[1,2,8,8192]{3,2,1,0:T(8,128)}), f32[64,2,8,8192]{3,2,1,0:T(8,128)}) %all-gather.11.cloned.1.call-update) | async-done | bytes 33554448 | tf_op jit(solution)/shard_map/all_gather | solution.py:65
  700.1 11.7 reduce_sum.19
  712.4 824.4 %all-reduce.3.cloned.1.call-done = f32[256,512]{1,0:T(8,128)} async-done(((f32[256,512]{1,0:T(8,128)}), f32[256,512]{1,0:T(8,128)}) %all-reduce.3.cloned.1.call-update) | async-done | bytes 524304
  1536.8 1.3 fusion.35
  (40 shorter events, 2.3 us)
Async XLA Ops:
  7.2 476.2 %all-gather.9.cloned.1.call-start = ((), (), s32[]{:S(2)}) async-start(), calls=%async_computation.1 | async-start | bytes 4718592 | tf_op jit(solution)/shard_map/all_gather | solution.py:50
  7.9 477.7 %all-gather.7.cloned.1.call-start = ((), (), s32[]{:S(2)}) async-start(), calls=%async_computation | async-start | bytes 4718592 | tf_op jit(solution)/shard_map/all_gather | solution.py:51
  8.6 691.4 %all-gather.11.cloned.1.call-start = ((), (), s32[]{:S(2)}) async-start(), calls=%async_computation.2 | async-start | bytes 34078720 | tf_op jit(solution)/shard_map/all_gather | solution.py:65
  192.9 2.0 copy-start.1
  194.6 172.8 %copy-start.2 = (f32[1,4,512]{2,1,0:T(4,128)S(1)}, f32[1,4,512]{2,1,0:T(4,128)}, u32[]{:S(2)}) copy-start(f32[1,4,512]{2,1,0:T(4,128)} %param.9) | copy-start | bytes 24580
  483.3 8.1 copy-start
  492.7 1044.1 %all-reduce.3.cloned.1.call-start = ((), (), s32[]{:S(2)}) async-start(), calls=%async_computation.3 | async-start | bytes 1048576
Sparse Core Ops, SparseCore 0:
  11.2 185.2 all-gather.8
  199.7 170.8 all-gather.6
  492.8 207.1 all-gather.10
  702.8 833.9 all-reduce.2
